TPU v7x, 32 devices: a whole 2x2x4 slice. The times are simulated.
32 devices in a mesh: dp: 8 (over z, x), cent: 4 (over y, core).
Axes of the slice: x: 2, y: 2, z: 4, core: 2. Of those that a mesh axis runs over, the one named last changes fastest.
Arguments:
- embeddings: bfloat16 [8192, 512], P('dp'), may hold values from -60 to 60, as said below
- centroids: bfloat16 [16384, 512], P('cent'), may hold values from -60 to 60, as said below
Outputs:
- new_centroids: float32 [16384, 512], P(('cent', 'dp'))
- column_mass: float32 [16384], P(('cent', 'dp'))
Inputs may be any that keep to these rules, and one draw needn't show every extreme that they name: `embeddings`: every row is nonzero. `centroids`: every row is nonzero.
All inputs are finite; a program needn't handle non-finite values.
Results may differ from a plain program's by a relative error of at most 0.00074.
Values sent between devices are 32-bit elements; how exact they have to be, the bound alone decides.
A program may use at most 128 MiB of HBM per device.

v0:
```python
import jax
import jax.numpy as jnp
from jax import lax
from jax.sharding import PartitionSpec as P

ITERS = 3


TAU = 0.02


def rms_rows(values):
    wide = values.astype(jnp.float32)
    return (wide * lax.rsqrt(jnp.mean(wide * wide, axis=1, keepdims=True) + 1e-06)).astype(
        jnp.bfloat16
    )


def column_total(weights, energy):
    partial_cols = jnp.dot(weights, energy, precision=lax.Precision.HIGHEST)
    return lax.psum(partial_cols, "dp")


def local(embeddings, centroids):
    high = lax.Precision.HIGHEST
    xh = rms_rows(embeddings)
    ch = rms_rows(centroids)
    width = xh.shape[1]
    local_rows = xh.shape[0]
    local_cents = ch.shape[0]
    n_data = lax.axis_size("dp")
    total_rows = float(local_rows * n_data)
    total_cents = float(local_cents * lax.axis_size("cent"))
    ratio = total_rows / total_cents
    scores = lax.dot_general(xh, ch, (((1,), (1,)), ((), ())), preferred_element_type=jnp.float32)
    energy = jnp.exp(scores * (1.0 / (TAU * width)))
    u = jnp.ones((local_rows,), jnp.float32)
    v = jnp.ones((local_cents,), jnp.float32)
    for step_index in range(ITERS):
        partial_rows = jnp.dot(energy, v, precision=high)
        rows_sum = lax.psum(partial_rows, "cent")
        cols = column_total(u, energy)
        u, v = (jnp.sqrt(u / rows_sum), jnp.sqrt(v * ratio / cols))
    cols = column_total(u, energy)
    plan = (total_cents * u[:, None] * energy * v[None, :]).astype(jnp.bfloat16)
    share = local_cents // n_data
    offset = lax.axis_index("dp") * share
    weighted = lax.dot_general(
        plan, xh, (((0,), (0,)), ((), ())), preferred_element_type=jnp.float32
    )
    summed = lax.psum(weighted, "dp")
    mine = lax.dynamic_slice_in_dim(summed, offset, share, 0)
    mass_all = v * cols * (total_cents / total_rows)
    column_mass = lax.dynamic_slice_in_dim(mass_all, offset, share, 0)
    new_centroids = mine * lax.rsqrt(jnp.mean(mine * mine, axis=1, keepdims=True) + 1e-06)
    return (new_centroids, column_mass)


def solution(mesh):
    in_specs = (P("dp", None), P("cent", None))
    out_specs = (P(("cent", "dp"), None), P(("cent", "dp")))
    return jax.shard_map(local, mesh=mesh, in_specs=in_specs, out_specs=out_specs, check_vma=False)
```

profile of v0, /device:TPU:0, one launch (start us, length us, event | category | flops | bytes accessed | tf_op | source)
XLA Modules:
  0.0 499.6 jit_solution(17064678215647114410)
XLA Ops:
  7.2 0.0 all-reduce.5.cloned.1.call-start
  7.2 1.5 fusion.7
  8.7 3.1 fusion
  11.8 7.3 %multiply_exponential_fusion = f32[1024,4096]{1,0:T(8,128)S(1)} fusion(bf16[4096,512]{1,0:T(8,128)(2,1)} %param.3, f32[4096]{0:T(1024)S(1)} %add_rsqrt_fusion, bf16[1024,512]{1,0:T(8,128)(2,1)} %param.2, f32[1024]{0:T(1024)S(1)} %add_rsqrt_fusion.1), kind=kOutput, calls=%fused_computation.1 | convolution fusion | flops 4307025920 | bytes 22040576 | tf_op jit(solution)/shard_map/dot_general | solution.py:35
  19.1 0.0 copy-start
  19.1 14.4 %fusion.11 = f32[1,1024]{1,0:T(1,128)S(1)} fusion(f32[1024,4096]{1,0:T(8,128)S(1)} %multiply_exponential_fusion), kind=kOutput, calls=%fused_computation.20 | convolution fusion | flops 50331648 | bytes 16781312 | tf_op jit(solution)/shard_map/dot_general | solution.py:40
  33.5 19.9 %fusion.14 = f32[1,4096]{1,0:T(1,128)S(1)} fusion(f32[1024,4096]{1,0:T(8,128)S(1)} %multiply_exponential_fusion), kind=kOutput, calls=%fused_computation.28 | convolution fusion | flops 50331648 | bytes 16793600 | tf_op jit(solution)/shard_map/dot_general | solution.py:20
  53.4 0.0 copy-done
  53.4 8.4 %psum.56 = f32[1024]{0:T(1024)S(1)} all-reduce(f32[1024]{0:T(1024)S(1)} %bitcast.32), channel_id=1, replica_groups=mesh['dp'=8,'cent'=4] {'cent'}, use_global_device_ids=true, to_apply=%region_2.0 | all-reduce | flops 1024 | bytes 8192 | tf_op jit(solution)/shard_map/psum | solution.py:41
  61.8 11.5 %fusion.19 = f32[1,4096]{1,0:T(1,128)S(1)} fusion(f32[1024,1]{0,1:T(1,128)S(1)} %bitcast.33, f32[1024,4096]{1,0:T(8,128)} %copy-done), kind=kOutput, calls=%fused_computation.35 | convolution fusion | flops 50331648 | bytes 16797696 | tf_op jit(solution)/shard_map/dot_general | solution.py:20
  73.3 37.4 %all-reduce.1 = (f32[4096]{0:T(1024)S(1)}, f32[4096]{0:T(1024)S(1)}) all-reduce(f32[4096]{0:T(1024)S(1)} %bitcast.25, f32[4096]{0:T(1024)S(1)} %bitcast.28), channel_id=1, replica_groups=mesh['dp'=8,'cent'=4] {'dp'}, use_global_device_ids=true, to_apply=%region_3.0 | all-reduce | flops 8192 | bytes 65536 | tf_op jit(solution)/shard_map/psum | solution.py:21
  110.7 17.6 %fusion.20 = f32[1,1024]{1,0:T(1,128)S(1)} fusion(f32[1024,4096]{1,0:T(8,128)} %copy-done, f32[4096,1]{0,1:T(1,128)S(1)} %bitcast.24), kind=kOutput, calls=%fused_computation.36 | convolution fusion | flops 50331648 | bytes 16797696 | tf_op jit(solution)/shard_map/dot_general | solution.py:40
  128.2 17.6 %fusion.18 = f32[1,1024]{1,0:T(1,128)S(1)} fusion(f32[1024,4096]{1,0:T(8,128)} %copy-done, f32[4096,1]{0,1:T(1,128)S(1)} %bitcast.26), kind=kOutput, calls=%fused_computation.34 | convolution fusion | flops 50331648 | bytes 16797696 | tf_op jit(solution)/shard_map/dot_general | solution.py:40
  145.8 6.2 %all-reduce.2 = (f32[1024]{0:T(1024)S(1)}, f32[1024]{0:T(1024)S(1)}) all-reduce(f32[1024]{0:T(1024)S(1)} %bitcast.31, f32[1024]{0:T(1024)S(1)} %bitcast.30), channel_id=1, replica_groups=mesh['dp'=8,'cent'=4] {'cent'}, use_global_device_ids=true, to_apply=%region_4.0 | all-reduce | flops 2048 | bytes 16384 | tf_op jit(solution)/shard_map/psum | solution.py:41
  152.0 0.0 copy-start.1
  152.1 11.5 %fusion.22 = f32[1,4096]{1,0:T(1,128)S(1)} fusion(f32[1024,1]{0,1:T(1,128)S(1)} %bitcast.35, f32[1024,4096]{1,0:T(8,128)} %copy-done), kind=kOutput, calls=%fused_computation.38 | convolution fusion | flops 50331648 | bytes 16797696 | tf_op jit(solution)/shard_map/dot_general | solution.py:20
  163.6 11.5 %fusion.21 = f32[1,4096]{1,0:T(1,128)S(1)} fusion(f32[1024,1]{0,1:T(1,128)S(1)} %bitcast.34, f32[1024,4096]{1,0:T(8,128)} %copy-done), kind=kOutput, calls=%fused_computation.37 | convolution fusion | flops 50331648 | bytes 16797696 | tf_op jit(solution)/shard_map/dot_general | solution.py:20
  175.1 33.3 %all-reduce = (f32[4096]{0:T(1024)S(1)}, f32[4096]{0:T(1024)S(1)}) all-reduce(f32[4096]{0:T(1024)S(1)} %bitcast.29, f32[4096]{0:T(1024)S(1)} %bitcast.27), channel_id=1, replica_groups=mesh['dp'=8,'cent'=4] {'dp'}, use_global_device_ids=true, to_apply=%region_7.0 | all-reduce | flops 8192 | bytes 65536 | tf_op jit(solution)/shard_map/psum | solution.py:21
  208.4 0.0 copy-done.1
  208.4 14.0 %fusion.2 = f32[4096,512]{1,0:T(8,128)} fusion(f32[1024,4096]{1,0:T(8,128)} %copy-done, f32[4096]{0:T(1024)S(1)} %divide_sqrt_fusion, f32[1024]{0:T(1024)S(1)} %get-tuple-element.8, bf16[1024,512]{1,0:T(8,128)(2,1)S(1)} %copy-done.1, f32[1024]{0:T(1024)S(1)} %add_rsqrt_fusion.1), kind=kOutput, calls=%fused_computation.6 | convolution fusion | flops 4309123072 | bytes 26238976 | tf_op jit(solution)/shard_map/dot_general | solution.py:48
  222.3 0.0 all-reduce.5.cloned.1.call-update
  222.4 0.7 fusion.13
  223.0 265.6 %all-reduce.5.cloned.1.call-done = f32[4096,512]{1,0:T(8,128)} async-done(((f32[4096,512]{1,0:T(8,128)}), f32[4096,512]{1,0:T(8,128)}) %all-reduce.5.cloned.1.call-update) | async-done | bytes 8388624 | tf_op jit(solution)/shard_map/psum | solution.py:51
  488.6 1.4 multiply_reduce_fusion
  490.0 2.3 dynamic-slice_multiply_fusion
  (7 shorter events, 0.1 us)
Async XLA Ops:
  7.2 481.4 %all-reduce.5.cloned.1.call-start = ((), (), s32[]{:S(2)}) async-start(), calls=%async_computation | async-start | bytes 16777216 | tf_op jit(solution)/shard_map/psum | solution.py:51
  19.1 34.3 %copy-start = (f32[1024,4096]{1,0:T(8,128)}, f32[1024,4096]{1,0:T(8,128)S(1)}, u32[]{:S(2)}) copy-start(f32[1024,4096]{1,0:T(8,128)S(1)} %multiply_exponential_fusion) | copy-start | bytes 50331652
  152.0 56.3 %copy-start.1 = (bf16[1024,512]{1,0:T(8,128)(2,1)S(1)}, bf16[1024,512]{1,0:T(8,128)(2,1)}, u32[]{:S(2)}) copy-start(bf16[1024,512]{1,0:T(8,128)(2,1)} %param.2) | copy-start | bytes 3145732
Sparse Core Ops, SparseCore 0:
  222.5 266.0 all-reduce.4
where the time goes:
time: 509 us; the launch traced here: 500 us
  waiting for transfers between devices  266 us (52%)
  matrix products  125 us (25%)
  blocking collectives  85.3 us (17%)
  between operations  14.6 us (3%)
  other arithmetic  9.04 us (2%)
    psum x1, waiting for transfers between devices, local(): summed = lax.psum(weighted, 'dp')  266 us
    psum x2, blocking collectives, column_total(): return lax.psum(partial_cols, 'dp')  70.7 us
    dot_general x4, matrix products, column_total(): partial_cols = jnp.dot(weights, energy, precision=lax.Precision.HIGHEST)  54.4 us
    dot_general x3, matrix products, local(): partial_rows = jnp.dot(energy, v, precision=high)  49.5 us
    psum x2, blocking collectives, local(): rows_sum = lax.psum(partial_rows, 'cent')  14.6 us
    dot_general x1, matrix products, local(): lax.dot_general(plan, xh, (((0,), (0,)), ((), ())), preferred_element_typ...  14 us
  transfers between devices with their start and end apart: 1, of which 1 were waited for; matrix products, arithmetic and copies ran while one was open for 0% of the time, Pallas kernels for 0%

commit v1 on v0

v1 whole, which is shorter than its diff:
```python
import functools
import jax
import jax.numpy as jnp
from jax import lax
from jax.experimental import pallas as pl
from jax.experimental.pallas import tpu as pltpu
from jax.sharding import PartitionSpec as P

ITERS = 3
TAU = 0.02
MESH = pl.DeviceIdType.MESH
NT = (((1,), (1,)), ((), ()))
NB = 8
CHUNK = 256


def rms_rows(values):
    wide = values.astype(jnp.float32)
    return (wide * lax.rsqrt(jnp.mean(wide * wide, axis=1, keepdims=True) + 1e-06)).astype(
        jnp.bfloat16
    )


def lane_tiles(values):
    total = values[:, :128]
    for t in range(1, values.shape[1] // 128):
        total = total + values[:, t * 128 : (t + 1) * 128]
    return total


def to_column(row):
    return jnp.broadcast_to(row, (128, row.shape[1])).T


def to_row(tile):
    return jnp.sum(tile.T, axis=0, keepdims=True)


def kernel(
    total_rows, total_cents, n_dp, n_cent,
    emb, cent, out_w, out_m,
    energy, ch, xg, xb, ucol, racc, cr, rr, uz, vv, ws, wr, cfs, cfr,
    c_send, c_recv, r_send, r_recv, z_send, z_recv, y_send, y_recv, k_send, k_recv,
    u_send, u_recv, w_send, w_recv,
):
    n_z = n_dp // 2
    rows, width = emb.shape
    cents = cent.shape[0]
    block = cents // NB
    quarter = rows // n_cent
    scale = 1.0 / (TAU * width)
    ratio = total_rows / total_cents
    d = lax.axis_index("dp")
    c = lax.axis_index("cent")
    z, x = d // 2, lax.rem(d, 2)
    y, core = c // 2, lax.rem(c, 2)
    dp_peers = [lax.rem(d + k, n_dp) for k in range(1, n_dp)]
    c_peers = [lax.rem(c + k, n_cent) for k in range(1, n_cent)]
    z_peers = [lax.rem(z + k, n_z) for k in range(1, n_z)]
    c_y = (1 - y) * 2 + core
    c_core = y * 2 + (1 - core)
    c_far = (1 - y) * 2 + (1 - core)
    d_x = z * 2 + (1 - x)

    barrier = pltpu.get_barrier_semaphore()
    for peer in dp_peers:
        pl.semaphore_signal(barrier, inc=1, device_id={"dp": peer, "cent": c}, device_id_type=MESH)
    for peer in c_peers:
        pl.semaphore_signal(barrier, inc=1, device_id={"dp": d, "cent": peer}, device_id_type=MESH)
    pl.semaphore_wait(barrier, n_dp - 1 + n_cent - 1)

    def remote(src, dst, ssem, rsem, dp, cn):
        return pltpu.make_async_remote_copy(
            src_ref=src, dst_ref=dst, send_sem=ssem, recv_sem=rsem,
            device_id={"dp": dp, "cent": cn}, device_id_type=MESH,
        )

    mine = pl.multiple_of(c * quarter, quarter)
    xg[z, c] = rms_rows(emb[pl.ds(mine, quarter), :]).astype(jnp.float32)

    def z_copy(k):
        return remote(
            xg.at[z, c], xg.at[z, c], z_send.at[k], z_recv.at[z], z_peers[k] * 2 + x, c
        )

    def z_arrival(k):
        src = z_peers[k]
        return remote(xg.at[src, c], xg.at[src, c], z_send.at[k], z_recv.at[src], d, c_y)

    def y_copy(k):
        src = z_peers[k]
        return remote(xg.at[src, c], xg.at[src, c], y_send.at[k], y_recv.at[src], d, c_y)

    def y_arrival(k):
        src = z_peers[k]
        return remote(xg.at[src, c_y], xg.at[src, c_y], y_send.at[k], y_recv.at[src], d, c_y)

    def k_copy(k, s, who):
        src = z_peers[k]
        return remote(
            xg.at[src, who], xg.at[src, who], k_send.at[k, s], k_recv.at[src, s], d, c_core
        )

    for k in range(n_z - 1):
        z_copy(k).start()

    base = pl.multiple_of(z * rows, rows)
    for i in range(n_cent):
        xb[pl.ds(base + i * quarter, quarter), :] = rms_rows(emb[i * quarter : (i + 1) * quarter, :])

    def exchange(it):
        rr[it, c] = to_row(racc[...])
        for k, peer in enumerate(dp_peers):
            remote(cr.at[it, d], cr.at[it, d], c_send.at[it, k], c_recv.at[it, d], peer, c).start()
        for k, peer in enumerate(c_peers):
            remote(rr.at[it, c], rr.at[it, c], r_send.at[it, k], r_recv.at[it, c], d, peer).start()
        for k, peer in enumerate(c_peers):
            got = remote(
                rr.at[it, peer], rr.at[it, peer], r_send.at[it, k], r_recv.at[it, peer], d, peer
            )
            got.wait()
        row_sum = rr[it, 0]
        for k in range(1, n_cent):
            row_sum = row_sum + rr[it, k]
        u_old = uz[z] if it else jnp.ones((1, rows), jnp.float32)
        u_new = jnp.sqrt(u_old / row_sum)
        uz[z] = u_new
        if it < ITERS - 1:
            ucol[...] = to_column(u_new)
        for k, peer in enumerate(dp_peers):
            got = remote(
                cr.at[it, peer], cr.at[it, peer], c_send.at[it, k], c_recv.at[it, peer], peer, c
            )
            got.wait()
        col_sum = cr[it, 0]
        for k in range(1, n_dp):
            col_sum = col_sum + cr[it, k]
        v_old = vv[...] if it else jnp.ones((NB, block), jnp.float32)
        vv[...] = jnp.sqrt(v_old * ratio / col_sum)

    racc[...] = jnp.zeros_like(racc)

    @pl.loop(0, NB)
    def _(b):
        at = pl.multiple_of(b * block, block)
        ch_b = rms_rows(cent[pl.ds(at, block), :])
        ch[pl.ds(at, block), :] = ch_b
        col = jnp.zeros((8, block), jnp.float32)
        for i in range(n_cent):
            part = slice(i * quarter, (i + 1) * quarter)
            s = lax.dot_general(
                xb[pl.ds(base + i * quarter, quarter), :], ch_b, NT,
                preferred_element_type=jnp.float32,
            )
            e = jnp.exp(s * scale)
            energy[b, part, :] = e
            racc[part, :] += lane_tiles(e)
            col = col + jnp.sum(e.reshape(quarter // 8, 8, block), axis=0)
        cr[0, d, pl.ds(b, 1), :] = jnp.sum(col, axis=0, keepdims=True)

    exchange(0)

    group = 64
    for it in range(1, ITERS):
        racc[...] = jnp.zeros_like(racc)

        @pl.loop(0, NB)
        def _(b):
            v_b = jnp.broadcast_to(vv[pl.ds(b, 1), :], (8, block))

            def step(g, col):
                r0 = pl.multiple_of(g * group, group)
                for i in range(group // 8):
                    e = energy[b, pl.ds(r0 + i * 8, 8), :]
                    u8 = ucol[pl.ds(r0 + i * 8, 8), :]
                    col = col + e * jnp.concatenate([u8] * (block // 128), axis=1)
                    racc[pl.ds(r0 + i * 8, 8), :] += lane_tiles(e * v_b)
                return col

            col = lax.fori_loop(0, rows // group, step, jnp.zeros((8, block), jnp.float32))
            cr[it, d, pl.ds(b, 1), :] = jnp.sum(col, axis=0, keepdims=True)

        exchange(it)

    def u_copy(k, owner):
        return remote(
            uz.at[owner], uz.at[owner], u_send.at[k], u_recv.at[owner], z_peers[k] * 2 + x, c
        )

    for k in range(n_z - 1):
        u_copy(k, z).start()
    for k in range(n_z - 1):
        z_copy(k).wait_send()
        z_arrival(k).wait_recv()
        y_copy(k).start()
        k_copy(k, 0, c).start()
    for k in range(n_z - 1):
        y_arrival(k).wait()
        k_copy(k, 1, c_y).start()
    for k in range(n_z - 1):
        k_copy(k, 0, c_core).wait()
        k_copy(k, 1, c_far).wait()
        u_copy(k, z_peers[k]).wait()
        src = z_peers[k]
        for i in range(n_cent):
            xb[pl.ds(pl.multiple_of(src * rows + i * quarter, quarter), quarter), :] = xg[
                src, i
            ].astype(jnp.bfloat16)

    def weigh(owner, s, dst):
        at = pl.multiple_of(owner * block + s * CHUNK, CHUNK)
        cc = ch[pl.ds(at, CHUNK), :]
        v_col = to_column(vv[pl.ds(owner, 1), :][:, s * CHUNK : (s + 1) * CHUNK])
        v_tile = jnp.concatenate([v_col] * (block // 128), axis=1)
        dst[s] = jnp.zeros((CHUNK, width), jnp.float32)

        def step(zz, acc):
            for h in range(rows // block):
                xr = xb[pl.ds(pl.multiple_of(zz * rows + h * block, block), block), :]
                u = uz[zz][:, h * block : (h + 1) * block]
                e = jnp.exp(
                    lax.dot_general(cc, xr, NT, preferred_element_type=jnp.float32) * scale
                )
                acc = acc + lane_tiles(e * u)
                q = ((total_cents * u) * e * v_tile).astype(jnp.bfloat16)
                dst[s] += jnp.dot(q, xr, preferred_element_type=jnp.float32)
            return acc

        acc = lax.fori_loop(0, n_z, step, jnp.zeros((CHUNK, 128), jnp.float32))
        return to_row(acc)

    n_s = block // CHUNK

    def w_copy(s):
        return remote(ws.at[s], wr.at[s], w_send.at[s], w_recv.at[s], d_x, c)

    for s in range(n_s):
        cfs[:, s * CHUNK : (s + 1) * CHUNK] = weigh(d_x, s, ws)
        w_copy(s).start()
    cf_copy = remote(cfs, cfr, w_send.at[n_s], w_recv.at[n_s], d_x, c)
    cf_copy.start()
    for s in range(n_s):
        out_m[:, s * CHUNK : (s + 1) * CHUNK] = weigh(d, s, out_w)
    for s in range(n_s):
        w_copy(s).wait()
        w = out_w[s] + wr[s]
        out_w[s] = w * lax.rsqrt(jnp.mean(w * w, axis=1, keepdims=True) + 1e-06)
    cf_copy.wait()
    out_m[...] = vv[pl.ds(d, 1), :] * (out_m[...] + cfr[...]) * (total_cents / total_rows)


def fused(embeddings, centroids):
    n_dp, n_cent = lax.axis_size("dp"), lax.axis_size("cent")
    rows, width = embeddings.shape
    cents = centroids.shape[0]
    n_z = n_dp // 2
    block = cents // NB
    quarter = rows // n_cent
    n_s = block // CHUNK
    f32 = jnp.float32
    dma = pltpu.SemaphoreType.DMA
    w, m = pl.pallas_call(
        functools.partial(
            kernel, float(rows * n_dp), float(cents * n_cent), n_dp, n_cent
        ),
        out_shape=(
            jax.ShapeDtypeStruct((n_s, CHUNK, width), f32),
            jax.ShapeDtypeStruct((1, block), f32),
        ),
        in_specs=[pl.BlockSpec(memory_space=pltpu.VMEM)] * 2,
        out_specs=(pl.BlockSpec(memory_space=pltpu.VMEM),) * 2,
        scratch_shapes=[
            pltpu.VMEM((NB, rows, block), f32),
            pltpu.VMEM((cents, width), jnp.bfloat16),
            pltpu.VMEM((n_z, n_cent, quarter, width), f32),
            pltpu.VMEM((n_z * rows, width), jnp.bfloat16),
            pltpu.VMEM((rows, 128), f32),
            pltpu.VMEM((rows, 128), f32),
            pltpu.VMEM((ITERS, n_dp, NB, block), f32),
            pltpu.VMEM((ITERS, n_cent, 1, rows), f32),
            pltpu.VMEM((n_z, 1, rows), f32),
            pltpu.VMEM((NB, block), f32),
            pltpu.VMEM((n_s, CHUNK, width), f32),
            pltpu.VMEM((n_s, CHUNK, width), f32),
            pltpu.VMEM((1, block), f32),
            pltpu.VMEM((1, block), f32),
            dma((ITERS, n_dp - 1)),
            dma((ITERS, n_dp)),
            dma((ITERS, n_cent - 1)),
            dma((ITERS, n_cent)),
            dma((n_z - 1,)),
            dma((n_z,)),
            dma((n_z - 1,)),
            dma((n_z,)),
            dma((n_z - 1, 2)),
            dma((n_z, 2)),
            dma((n_z - 1,)),
            dma((n_z,)),
            dma((n_s + 1,)),
            dma((n_s + 1,)),
        ],
        compiler_params=pltpu.CompilerParams(
            collective_id=0, has_side_effects=True, vmem_limit_bytes=60 * 2**20
        ),
    )(embeddings, centroids)
    return w.reshape(block, width), m.reshape(block)


def column_total(weights, energy):
    return lax.psum(jnp.dot(weights, energy, precision=lax.Precision.HIGHEST), "dp")


def local(embeddings, centroids):
    n_data = lax.axis_size("dp")
    xh = rms_rows(embeddings)
    ch = rms_rows(centroids)
    local_rows, width = xh.shape
    local_cents = ch.shape[0]
    total_rows = float(local_rows * n_data)
    total_cents = float(local_cents * lax.axis_size("cent"))
    scores = lax.dot_general(xh, ch, NT, preferred_element_type=jnp.float32)
    energy = jnp.exp(scores * (1.0 / (TAU * width)))
    u = jnp.ones((local_rows,), jnp.float32)
    v = jnp.ones((local_cents,), jnp.float32)
    for step_index in range(ITERS):
        rows_sum = lax.psum(jnp.dot(energy, v, precision=lax.Precision.HIGHEST), "cent")
        cols = column_total(u, energy)
        u, v = (jnp.sqrt(u / rows_sum), jnp.sqrt(v * (total_rows / total_cents) / cols))
    cols = column_total(u, energy)
    plan = (total_cents * u[:, None] * energy * v[None, :]).astype(jnp.bfloat16)
    share = local_cents // n_data
    weighted = lax.dot_general(
        plan, xh, (((0,), (0,)), ((), ())), preferred_element_type=jnp.float32
    )
    mine = lax.psum_scatter(weighted, "dp", scatter_dimension=0, tiled=True)
    mass_all = v * cols * (total_cents / total_rows)
    column_mass = lax.dynamic_slice_in_dim(mass_all, lax.axis_index("dp") * share, share, 0)
    new_centroids = mine * lax.rsqrt(jnp.mean(mine * mine, axis=1, keepdims=True) + 1e-06)
    return (new_centroids, column_mass)


def solution(mesh):
    in_specs = (P("dp", None), P("cent", None))
    out_specs = (P(("cent", "dp"), None), P(("cent", "dp")))
    small = mesh.shape["dp"] == NB and mesh.shape["cent"] == 4
    body = fused if small else local
    return jax.shard_map(body, mesh=mesh, in_specs=in_specs, out_specs=out_specs, check_vma=False)
```

time: 509 us -> 145 us (0.28); the launches traced: 500 us -> 145 us
  waiting for transfers between devices: 266 us -> 0 us
  Pallas kernels: 0 us -> 140 us
  matrix products: 125 us -> 0 us
  blocking collectives: 85.3 us -> 0 us
  between operations: 14.6 us -> 0.64 us
  other arithmetic: 9.04 us -> 0 us
    psum x1 -> x0, waiting for transfers between devices: 266 us -> none  [local(): summed = lax.psum(weighted, 'dp')]
    pallas_call x0 -> x1, Pallas kernels: none -> 140 us  [fused(): pl.pallas_call(functools.partial(kernel, float(rows * n_dp), float(cents...]
    dot_general x9 -> x0, matrix products: 125 us -> none  [the longest x4 54.4 us: column_total(): partial_cols = jnp.dot(weights, energy, precision=lax.Precision.HIGHEST)]
    psum x4 -> x0, blocking collectives: 85.3 us -> none  [the longest x2 70.7 us: column_total(): return lax.psum(partial_cols, 'dp')]
    reduce_sum x3 -> x0, other arithmetic: 5.96 us -> none  [the longest x2 4.58 us: rms_rows(): jnp.mean(wide * wide, axis=1, keepdims=True) + 1e-06]
  transfers between devices with their start and end apart: 1 -> 0, of which waited for: 1 -> 0; matrix products, arithmetic and copies ran while one was open for 0% -> 0% of each run, Pallas kernels for 0% -> 0%
where the time goes in v1:
time: 145 us
  Pallas kernels  140 us (97%)
  local copies, waits for them, and re-layouts  3.52 us (2%)
    pallas_call x1, Pallas kernels, fused(): pl.pallas_call(functools.partial(kernel, float(rows * n_dp), float(cents...  140 us
    unnamed x2, local copies, waits for them, and re-layouts  3.52 us

profile of v1, /device:TPU:0, one launch (start us, length us, event | category | flops | bytes accessed | tf_op | source)
XLA Modules:
  0.0 144.6 jit_solution(17315201794050103475)
XLA Ops:
  0.6 140.5 %shard_map.41 = (f32[2,256,512]{2,1,0:T(8,128)}, f32[1,512]{1,0:T(1,128)}) custom-call(bf16[1024,512]{1,0:T(8,128)(2,1)} %emb.1, bf16[4096,512]{1,0:T(8,128)(2,1)} %cent.1), custom_call_target="tpu_custom_call" | custom-call | tf_op jit(solution)/shard_map/pallas_call | solution.py:262
  141.1 2.3 %copy.6 = f32[512,512]{1,0:T(8,128)} copy(f32[512,512]{1,0:T(8,128)} %bitcast.2) | data formatting | bytes 2097152
  143.4 1.3 copy.7

commit v2 on v1

--- a/solution.py
+++ b/solution.py
@@ -78,31 +78,73 @@
     mine = pl.multiple_of(c * quarter, quarter)
     xg[z, c] = rms_rows(emb[pl.ds(mine, quarter), :]).astype(jnp.float32)
 
-    def z_copy(k):
+    low = z // 2
+    first = z + 1 - 2 * low
+    last = 3 - 3 * low
+    order = [first, 6 - z - first - last, last]
+    middle = (z == 1) | (z == 2)
+
+    def z_copy(src, to, sem):
         return remote(
-            xg.at[z, c], xg.at[z, c], z_send.at[k], z_recv.at[z], z_peers[k] * 2 + x, c
+            xg.at[src, c], xg.at[src, c], z_send.at[sem], z_recv.at[src], to * 2 + x, c
         )
 
-    def z_arrival(k):
-        src = z_peers[k]
-        return remote(xg.at[src, c], xg.at[src, c], z_send.at[k], z_recv.at[src], d, c_y)
-
-    def y_copy(k):
-        src = z_peers[k]
-        return remote(xg.at[src, c], xg.at[src, c], y_send.at[k], y_recv.at[src], d, c_y)
-
-    def y_arrival(k):
-        src = z_peers[k]
-        return remote(xg.at[src, c_y], xg.at[src, c_y], y_send.at[k], y_recv.at[src], d, c_y)
-
-    def k_copy(k, s, who):
-        src = z_peers[k]
+    def z_arrival(src):
+        z_copy(src, first, 0).wait_recv()
+
+    def relay(src):
+        to = jnp.where(src > z, z - 1, z + 1)
+        return z_copy(src, to, src)
+
+    def y_copy(src, who):
+        return remote(xg.at[src, who], xg.at[src, who], y_send.at[src], y_recv.at[src], d, c_y)
+
+    def k_copy(src, s, who):
         return remote(
-            xg.at[src, who], xg.at[src, who], k_send.at[k, s], k_recv.at[src, s], d, c_core
+            xg.at[src, who], xg.at[src, who], k_send.at[src, s], k_recv.at[src, s], d, c_core
         )
 
-    for k in range(n_z - 1):
-        z_copy(k).start()
+    def forward(j):
+        if j == 0:
+            z_arrival(order[0])
+
+            @pl.when(middle)
+            def _():
+                relay(order[0]).start()
+                z_arrival(order[1])
+                relay(order[1]).start()
+
+        if j == 1:
+
+            @pl.when(jnp.logical_not(middle))
+            def _():
+                z_arrival(order[1])
+
+        if j == 2:
+
+            @pl.when(jnp.logical_not(middle))
+            def _():
+                z_arrival(order[2])
+
+        if j < 3:
+            y_copy(order[j], c).start()
+            k_copy(order[j], 0, c).start()
+        if j == 1:
+
+            @pl.when(middle)
+            def _():
+                z_arrival(order[2])
+                relay(order[2]).start()
+
+        if j > 0:
+            y_copy(order[j - 1], c_y).wait()
+            k_copy(order[j - 1], 1, c_y).start()
+
+    z_copy(z, first, z).start()
+
+    @pl.when(middle)
+    def _():
+        z_copy(z, 2 * z - first, n_z).start()
 
     base = pl.multiple_of(z * rows, rows)
     for i in range(n_cent):
@@ -114,6 +156,8 @@
             remote(cr.at[it, d], cr.at[it, d], c_send.at[it, k], c_recv.at[it, d], peer, c).start()
         for k, peer in enumerate(c_peers):
             remote(rr.at[it, c], rr.at[it, c], r_send.at[it, k], r_recv.at[it, c], d, peer).start()
+        if it < ITERS - 1:
+            forward(it + 1)
         for k, peer in enumerate(c_peers):
             got = remote(
                 rr.at[it, peer], rr.at[it, peer], r_send.at[it, k], r_recv.at[it, peer], d, peer
@@ -142,6 +186,10 @@
 
     @pl.loop(0, NB)
     def _(b):
+        @pl.when(b == 5)
+        def _():
+            forward(0)
+
         at = pl.multiple_of(b * block, block)
         ch_b = rms_rows(cent[pl.ds(at, block), :])
         ch[pl.ds(at, block), :] = ch_b
@@ -189,17 +237,19 @@
 
     for k in range(n_z - 1):
         u_copy(k, z).start()
+    forward(3)
+    z_copy(z, first, z).wait_send()
+
+    @pl.when(middle)
+    def _():
+        z_copy(z, 2 * z - first, n_z).wait_send()
+        for src in order:
+            relay(src).wait_send()
+
+    for k, src in enumerate(order):
+        k_copy(src, 0, c_core).wait()
+        k_copy(src, 1, c_far).wait()
     for k in range(n_z - 1):
-        z_copy(k).wait_send()
-        z_arrival(k).wait_recv()
-        y_copy(k).start()
-        k_copy(k, 0, c).start()
-    for k in range(n_z - 1):
-        y_arrival(k).wait()
-        k_copy(k, 1, c_y).start()
-    for k in range(n_z - 1):
-        k_copy(k, 0, c_core).wait()
-        k_copy(k, 1, c_far).wait()
         u_copy(k, z_peers[k]).wait()
         src = z_peers[k]
         for i in range(n_cent):
@@ -288,11 +338,11 @@
             dma((ITERS, n_dp)),
             dma((ITERS, n_cent - 1)),
             dma((ITERS, n_cent)),
-            dma((n_z - 1,)),
+            dma((n_z + 1,)),
             dma((n_z,)),
-            dma((n_z - 1,)),
             dma((n_z,)),
-            dma((n_z - 1, 2)),
+            dma((n_z,)),
+            dma((n_z, 2)),
             dma((n_z, 2)),
             dma((n_z - 1,)),
             dma((n_z,)),

time: 145 us -> 96.8 us (0.67)
  Pallas kernels: 140 us -> 92.5 us
    pallas_call x1, Pallas kernels: 140 us -> 92.5 us  [fused(): pl.pallas_call(functools.partial(kernel, float(rows * n_dp), float(cents...]
where the time goes in v2:
time: 96.8 us; the launch traced here: 96.6 us
  Pallas kernels  92.5 us (96%)
  local copies, waits for them, and re-layouts  3.52 us (4%)
    pallas_call x1, Pallas kernels, fused(): pl.pallas_call(functools.partial(kernel, float(rows * n_dp), float(cents...  92.5 us
    unnamed x2, local copies, waits for them, and re-layouts  3.52 us

profile of v2, /device:TPU:0, one launch (start us, length us, event | category | flops | bytes accessed | tf_op | source)
XLA Modules:
  0.0 96.6 jit_solution(5381452933386063380)
XLA Ops:
  0.6 92.5 %shard_map.41 = (f32[2,256,512]{2,1,0:T(8,128)}, f32[1,512]{1,0:T(1,128)}) custom-call(bf16[1024,512]{1,0:T(8,128)(2,1)} %emb.1, bf16[4096,512]{1,0:T(8,128)(2,1)} %cent.1), custom_call_target="tpu_custom_call" | custom-call | tf_op jit(solution)/shard_map/pallas_call | solution.py:312
  93.1 2.3 %copy.6 = f32[512,512]{1,0:T(8,128)} copy(f32[512,512]{1,0:T(8,128)} %bitcast.2) | data formatting | bytes 2097152
  95.4 1.3 %copy.7 = f32[512]{0:T(512)} copy(f32[512]{0:T(512)} %bitcast.3) | data formatting | bytes 4096
